TPU v7x, 32 devices: a whole 2x2x4 slice. The times are simulated.
32 devices in a mesh: ctx: 8 (over z, x), head: 4 (over y, core).
Axes of the slice: x: 2, y: 2, z: 4, core: 2. Of those that a mesh axis runs over, the one named last changes fastest.
Arguments:
- q_latent: bfloat16 [1024, 1536], P('ctx'), may hold values from -6 to 6
- latent_bias: float32 [8, 1536], P('ctx'), may hold values from -3 to 3
- norm_gain: float32 [1536], replicated, may hold values from 0.5 to 1.5
- w_q: bfloat16 [1536, 24576], P('ctx', 'head'), may hold values from -0.15625 to 0.15625
- steer: float32 [8, 24576], P('ctx', 'head'), may hold values from -10 to 10
- kv_latent: bfloat16 [1024, 512], P('ctx'), may hold values from -6 to 6
- key_rope: bfloat16 [1024, 64], P('ctx'), may hold values from -10 to 10
- w_uk: bfloat16 [512, 16384], P(None, 'head'), may hold values from -0.25 to 0.25
- w_uv: bfloat16 [512, 16384], P(None, 'head'), may hold values from -0.25 to 0.25
- d_out: bfloat16 [1024, 16384], P('ctx', 'head'), may hold values from -0.29882812 to 0.29882812
- block_mask: int32 [8, 8], replicated, may hold values from 0 to 1, as said below
Outputs:
- grad_steer: float32 [8, 24576], P('ctx', 'head')
- grad_latent_bias: float32 [8, 1536], P('ctx')
Inputs may be any that keep to these rules, and one draw needn't show every extreme that they name: `block_mask`: query block i always attends key block i; its other entries are 1 at a rate drawn per query block among 1/16, 2/16, 4/16 and 7/16.
All inputs are finite; a program needn't handle non-finite values.
Results may differ from a plain program's by a relative error of at most 0.024.
Values may be sent and summed in bfloat16 or wider, within the bound.
No kernel may reach another device: no remote copies, remote signals or barrier semaphores. Data moves between devices by JAX's collectives and lax.ppermute only.
A program may use at most 128 MiB of HBM per device.

v0:
```python
import math
import jax
import jax.numpy as jnp
from jax import lax
from jax.sharding import PartitionSpec as P

KVL = 512
NOPE = 128
ROPE = 64
VD = 128
BLK = 128
epsilon = 1e-06
lowest = -1e30


def contract_last(left, right):
    return lax.dot_general(
        left, right, (((1,), (1,)), ((), ())), preferred_element_type=jnp.float32
    )


def shards(
    q_latent, latent_bias, norm_gain, w_q, steer, kv_latent, key_rope, w_uk, w_uv, d_out, block_mask
):
    queries = q_latent.shape[0]
    nblocks = queries // BLK
    head_count = w_uk.shape[1] // NOPE
    head_width = NOPE + ROPE
    score_scale = head_width ** (-0.5)
    row_count = queries * head_count
    shifted = q_latent.astype(jnp.float32) + jnp.repeat(latent_bias, BLK, axis=0)
    inv_rms = lax.rsqrt(jnp.mean(shifted * shifted, axis=1, keepdims=True) + epsilon)
    normed = shifted * inv_rms
    c_query = (normed * norm_gain).astype(jnp.bfloat16)
    full_wq = lax.all_gather(w_q, "ctx", axis=0, tiled=True)
    projected = jnp.dot(c_query, full_wq, preferred_element_type=jnp.float32)
    query_all = (
        (projected + jnp.repeat(steer, BLK, axis=0))
        .astype(jnp.bfloat16)
        .reshape(queries, head_count, head_width)
    )
    q_rope = query_all[:, :, NOPE:].reshape(row_count, ROPE)
    key_up = w_uk.reshape(KVL, head_count, NOPE)
    value_up = w_uv.reshape(KVL, head_count, VD)
    q_absorbed = (
        jnp.einsum(
            "qhn,khn->qhk", query_all[:, :, :NOPE], key_up, preferred_element_type=jnp.float32
        )
        .astype(jnp.bfloat16)
        .reshape(row_count, KVL)
    )
    g_absorbed = (
        jnp.einsum(
            "qhv,khv->qhk",
            d_out.reshape(queries, head_count, VD),
            value_up,
            preferred_element_type=jnp.float32,
        )
        .astype(jnp.bfloat16)
        .reshape(row_count, KVL)
    )
    my_mask = lax.dynamic_slice_in_dim(block_mask, lax.axis_index("ctx") * nblocks, nblocks, 0)
    start_status = (
        jnp.full((row_count,), lowest, jnp.float32),
        jnp.zeros((row_count,), jnp.float32),
        jnp.zeros((row_count,), jnp.float32),
        jnp.zeros((2 * row_count, KVL), jnp.float32),
        jnp.zeros((2 * row_count, ROPE), jnp.float32),
    )
    lat_portion = lax.all_gather(kv_latent, "ctx", axis=0, tiled=True)
    rope_portion = lax.all_gather(key_rope, "ctx", axis=0, tiled=True)
    key_total = lat_portion.shape[0]
    tile_len = math.gcd(key_total, BLK)
    tile_count = key_total // tile_len

    def visit_tile(status, inputs):
        lat_tile, rope_tile, offset = inputs
        key_block = offset * tile_len // BLK
        column = lax.dynamic_index_in_dim(my_mask, key_block, 1, keepdims=False)

        def update(status):
            peak, total_weight, weighted, lat_acc, rope_acc = status
            live_rows = jnp.repeat(column > 0, head_count * BLK)[:, None]
            scores = (
                contract_last(q_absorbed, lat_tile) + contract_last(q_rope, rope_tile)
            ) * score_scale
            scores = jnp.where(live_rows, scores, lowest)
            new_peak = jnp.maximum(peak, jnp.max(scores, axis=1))
            factor = jnp.exp(peak - new_peak)
            weights = jnp.where(live_rows, jnp.exp(scores - new_peak[:, None]), 0.0)
            dots = contract_last(g_absorbed, lat_tile)
            mixed = weights * dots
            total_weight = total_weight * factor + jnp.sum(weights, axis=1)
            weighted = weighted * factor + jnp.sum(mixed, axis=1)
            stacked = jnp.concatenate([mixed, weights], axis=0).astype(jnp.bfloat16)
            doubled = jnp.concatenate([factor, factor])[:, None]
            lat_acc = lat_acc * doubled + jnp.dot(
                stacked, lat_tile, preferred_element_type=jnp.float32
            )
            rope_acc = rope_acc * doubled + jnp.dot(
                stacked, rope_tile, preferred_element_type=jnp.float32
            )
            return (new_peak, total_weight, weighted, lat_acc, rope_acc)

        def keep_status(status):
            return status

        return (lax.cond(jnp.max(column) > 0, update, keep_status, status), None)

    offsets = jnp.arange(tile_count, dtype=jnp.int32)
    tiles = (
        lat_portion.reshape(tile_count, tile_len, KVL),
        rope_portion.reshape(tile_count, tile_len, ROPE),
        offsets,
    )
    result, unused = lax.scan(visit_tile, start_status, tiles)
    peak, total_weight, weighted, lat_acc, rope_acc = result
    ratio = (weighted / total_weight)[:, None]
    inverse = (score_scale / total_weight)[:, None]
    grad_lat = ((lat_acc[:row_count] - ratio * lat_acc[row_count:]) * inverse).astype(jnp.bfloat16)
    grad_rope = (rope_acc[:row_count] - ratio * rope_acc[row_count:]) * inverse
    grad_nope = jnp.einsum(
        "qhk,khn->qhn",
        grad_lat.reshape(queries, head_count, KVL),
        key_up,
        preferred_element_type=jnp.float32,
    )
    grad_query = jnp.concatenate(
        [grad_nope, grad_rope.reshape(queries, head_count, ROPE)], axis=2
    ).reshape(queries, head_count * head_width)
    grad_steer = jnp.sum(grad_query.reshape(nblocks, BLK, head_count * head_width), axis=1)
    grad_round = grad_query.astype(jnp.bfloat16)
    partial_grad = contract_last(grad_round, full_wq)
    latent_grad = lax.psum(partial_grad.astype(jnp.bfloat16), "head").astype(jnp.float32)
    scaled = latent_grad * norm_gain
    project_mean = jnp.mean(scaled * normed, axis=1, keepdims=True)
    grad_shifted = inv_rms * (scaled - normed * project_mean)
    grad_bias = jnp.sum(grad_shifted.reshape(nblocks, BLK, grad_shifted.shape[1]), axis=1)
    return (grad_steer, grad_bias)


def solution(mesh):
    in_specs = (
        P("ctx", None),
        P("ctx", None),
        P(),
        P("ctx", "head"),
        P("ctx", "head"),
        P("ctx", None),
        P("ctx", None),
        P(None, "head"),
        P(None, "head"),
        P("ctx", "head"),
        P(),
    )
    out_specs = (P("ctx", "head"), P("ctx", None))
    return jax.shard_map(shards, mesh=mesh, in_specs=in_specs, out_specs=out_specs, check_vma=False)
```

profile of v0, /device:TPU:0, one launch (start us, length us, event | category | flops | bytes accessed | tf_op | source)
XLA Modules:
  0.0 604.1 jit_solution(11395170812251532337)
XLA Ops:
  7.2 0.7 all-gather.5.cloned.1.call-update
  8.0 0.7 all-gather.3.cloned.1.call-update
  8.7 54.1 %all_gather.11 = bf16[1024,64]{0,1:T(8,128)(2,1)S(1)} all-gather(bf16[128,64]{0,1:T(8,128)(2,1)} %param.21), channel_id=1, replica_groups=mesh['ctx'=8,'head'=4] {'ctx'}, dimensions={0}, use_global_device_ids=true | all-gather | bytes 147456 | tf_op jit(solution)/shard_map/all_gather | solution.py:71
  62.9 6.5 %copy.46 = bf16[512,4096]{0,1:T(8,128)(2,1)} copy(bf16[512,4096]{1,0:T(8,128)(2,1)} %param.22) | data formatting | bytes 8388608 | tf_op jit(solution)/shard_map/reshape | solution.py:43
  69.4 3.5 convert_bitcast_fusion.1
  73.0 4.4 copy.40
  77.6 0.7 constant_dynamic-slice_fusion.1
  78.3 298.5 %all-gather.5.cloned.1.call-done = bf16[1536,6144]{1,0:T(8,128)(2,1)} async-done(((bf16[192,6144]{1,0:T(8,128)(2,1)}), bf16[1536,6144]{1,0:T(8,128)(2,1)}) %all-gather.5.cloned.1.call-update) | async-done | bytes 18874384 | tf_op jit(solution)/shard_map/all_gather | solution.py:35
  376.8 10.2 %fusion.23 = bf16[128,6144]{1,0:T(8,128)(2,1)} fusion(bf16[1536,6144]{1,0:T(8,128)(2,1)} %all-gather.5.cloned.1.call-done, f32[6144]{0:T(1024)S(1)} %bitcast.78, bf16[128,1536]{1,0:T(8,128)(2,1)S(1)} %copy-done.5, f32[1536]{0:T(1024)S(1)} %copy-done.9, f32[128]{0:T(128)S(1)} %add_rsqrt_fusion, f32[1536]{0:T(1024)S(1)} %reduce.7), kind=kOutput, calls=%fused_computation.37 | convolution fusion | flops 2418475008 | bytes 20877824 | tf_op jit(solution)/shard_map/dot_general | solution.py:36
  387.0 2.1 copy.32
  389.2 2.5 copy.37
  391.7 3.5 convert_bitcast_fusion.2
  395.2 4.5 copy.35
  399.7 18.9 %all-gather.3.cloned.1.call-done = bf16[1024,512]{1,0:T(8,128)(2,1)} async-done(((bf16[128,512]{1,0:T(8,128)(2,1)}), bf16[1024,512]{1,0:T(8,128)(2,1)}) %all-gather.3.cloned.1.call-update) | async-done | bytes 1048592 | tf_op jit(solution)/shard_map/all_gather | solution.py:70
  418.8 7.9 %broadcast_in_dim.47 = f32[8192,512]{1,0:T(8,128)} broadcast(f32[]{:T(128)} %constant.105.clone.1), dimensions={} | broadcast | bytes 16777220 | tf_op jit(solution)/shard_map/broadcast_in_dim | solution.py:67
  426.7 62.8 %while.20 = (s32[]{:T(128)}, f32[4096]{0:T(1024)S(1)}, f32[4096]{0:T(1024)S(1)}, f32[4096]{0:T(1024)S(1)}, f32[8192,512]{1,0:T(8,128)}, /*index=5*/f32[8192,64]{...) while((s32[]{:T(128)}, f32[4096]{0:T(1024)S(1)}, ...), condition=%wide.region_7.8_spmd, body=%wide.region_1.7_spmd.sunk | while | flops 2372423680 | bytes 79006344 | solution.py:116
  427.9 0.6 fusion.59
  429.2 21.2 %conditional.2 = ((f32[4096]{0:T(1024)S(1)}, f32[4096]{0:T(1024)S(1)}, f32[4096]{0:T(1024)S(1)}, f32[8192,512]{1,0:T(8,128)}, f32[8192,64]{0,1:T(8,128)S(1)})) conditional(s32[]{:T(128)} %bitcast.67, (f32[4096]{0:T(1024)S(1)}, f32[4096]{0:T(1024)S(1)}, f32[4096]{0:T(1024)S(1)}, f32[8192,512]{1,0:T(8,128)}, f32[8192,64]{0,1:T(8,128)S(1)}) %tuple.55, ...), branch_computations={%region_2.2_spmd, %region_3.6_spmd} | conditional | flops 2372423680 | bytes 79005792 | solution.py:108
  429.8 3.7 fusion.7
  433.6 1.9 fusion.43
  436.1 2.5 fusion.4
  438.6 0.9 convolution_add_fusion
  439.5 10.9 %multiply_add_fusion = f32[8192,512]{1,0:T(8,128)} fusion(f32[8192,512]{1,0:T(8,128)} %get-tuple-element.261, f32[8192]{0:T(1024)S(1)} %pad_maximum_fusion.3, bf16[4096,128]{0,1:T(8,128)(2,1)S(1)} %get-tuple-element.320, bf16[4096,128]{0,1:T(8,128)(2,1)S(1)} %get-tuple-element.327, bf16[8,128,512]{2,1,0:T(8,128)(2,1)} %get-tuple-element.253, ...), kind=kOutput, calls=%fused_computation | convolution fusion | flops 1086324736 | bytes 35815936 | tf_op jit(solution)/shard_map/while/body/eval_jaxpr/cond/branch_1_fun/dot_general | solution.py:97
  451.7 0.6 fusion.59
  454.2 0.6 fusion.59
  456.8 0.6 fusion.59
  459.4 0.6 fusion.59
  461.9 0.6 fusion.59
  464.5 0.6 fusion.59
  465.8 21.2 %conditional.2 = ((f32[4096]{0:T(1024)S(1)}, f32[4096]{0:T(1024)S(1)}, f32[4096]{0:T(1024)S(1)}, f32[8192,512]{1,0:T(8,128)}, f32[8192,64]{0,1:T(8,128)S(1)})) conditional(s32[]{:T(128)} %bitcast.67, (f32[4096]{0:T(1024)S(1)}, f32[4096]{0:T(1024)S(1)}, f32[4096]{0:T(1024)S(1)}, f32[8192,512]{1,0:T(8,128)}, f32[8192,64]{0,1:T(8,128)S(1)}) %tuple.55, ...), branch_computations={%region_2.2_spmd, %region_3.6_spmd} | conditional | flops 2372423680 | bytes 79005792 | solution.py:108
  466.4 3.7 fusion.7
  470.2 1.9 fusion.43
  472.7 2.5 fusion.4
  475.2 0.9 convolution_add_fusion
  476.1 10.9 %multiply_add_fusion = f32[8192,512]{1,0:T(8,128)} fusion(f32[8192,512]{1,0:T(8,128)} %get-tuple-element.261, f32[8192]{0:T(1024)S(1)} %pad_maximum_fusion.3, bf16[4096,128]{0,1:T(8,128)(2,1)S(1)} %get-tuple-element.320, bf16[4096,128]{0,1:T(8,128)(2,1)S(1)} %get-tuple-element.327, bf16[8,128,512]{2,1,0:T(8,128)(2,1)} %get-tuple-element.253, ...), kind=kOutput, calls=%fused_computation | convolution fusion | flops 1086324736 | bytes 35815936 | tf_op jit(solution)/shard_map/while/body/eval_jaxpr/cond/branch_1_fun/dot_general | solution.py:97
  488.2 0.6 fusion.59
  489.5 6.9 %multiply_convert_fusion = bf16[4096,512]{1,0:T(8,128)(2,1)S(1)} fusion(f32[8192,512]{1,0:T(8,128)} %get-tuple-element.288, f32[4096]{0:T(1024)S(1)} %get-tuple-element.331, f32[4096]{0:T(1024)S(1)} %get-tuple-element.330), kind=kLoop, calls=%fused_computation.35 | loop fusion | flops 8388608 | bytes 21004288 | tf_op jit(solution)/shard_map/convert_element_type | solution.py:120
  496.6 2.8 fusion.33
  499.3 1.9 copy.43
  501.3 2.7 copy.44
  503.9 1.0 copy-done.4
  504.9 1.4 fusion.31
  506.3 14.1 %convolution_convert_fusion = bf16[128,1536]{1,0:T(8,128)(2,1)} fusion(bf16[128,6144]{0,1:T(8,128)(2,1)} %bitcast.76, bf16[1536,6144]{1,0:T(8,128)(2,1)} %all-gather.5.cloned.1.call-done), kind=kOutput, calls=%fused_computation.48 | convolution fusion | flops 2416115712 | bytes 20840448 | tf_op jit(solution)/shard_map/dot_general | solution.py:17
  520.5 3.0 fusion.32
  523.5 1.5 reduce_sum.64
  524.9 69.5 %all-reduce.2.cloned.1.call-done = bf16[128,1536]{1,0:T(8,128)(2,1)} async-done(((bf16[128,1536]{1,0:T(8,128)(2,1)}), bf16[128,1536]{1,0:T(8,128)(2,1)}) %all-reduce.2.cloned.1.call-update) | async-done | bytes 393232 | tf_op jit(solution)/shard_map/psum | solution.py:134
  594.4 1.3 multiply_reduce_fusion.1
  595.7 1.3 multiply_reduce_fusion
  (71 shorter events, 7.7 us)
Async XLA Ops:
  7.2 62.3 %copy-start = (bf16[128,4096]{1,0:T(8,128)(2,1)S(1)}, bf16[128,4096]{1,0:T(8,128)(2,1)}, u32[]{:S(2)}) copy-start(bf16[128,4096]{1,0:T(8,128)(2,1)} %param.24) | copy-start | bytes 3145732
  7.2 369.6 %all-gather.5.cloned.1.call-start = ((), (), s32[]{:S(2)}) async-start(), calls=%async_computation.1 | async-start | bytes 21233664 | tf_op jit(solution)/shard_map/all_gather | solution.py:35
  7.9 410.7 %all-gather.3.cloned.1.call-start = ((), (), s32[]{:S(2)}) async-start(), calls=%async_computation | async-start | bytes 1179648 | tf_op jit(solution)/shard_map/all_gather | solution.py:70
  8.7 585.8 %all-reduce.2.cloned.1.call-start = ((), (), s32[]{:S(2)}) async-start(), calls=%async_computation.2 | async-start | bytes 786432 | tf_op jit(solution)/shard_map/psum | solution.py:134
  73.0 4.4 copy-start.13
  73.0 4.4 copy-start.5
  73.0 303.8 %copy-start.9 = (f32[1536]{0:T(1024)S(1)}, f32[1536]{0:T(1024)}, u32[]{:S(2)}) copy-start(f32[1536]{0:T(1024)} %param.17) | copy-start | bytes 18436
  73.0 303.8 %copy-start.11 = (f32[1,6144]{1,0:T(1,128)S(1)}, f32[1,6144]{1,0:T(1,128)}, u32[]{:S(2)}) copy-start(f32[1,6144]{1,0:T(1,128)} %param.19) | copy-start | bytes 73732
  77.4 309.6 %copy-start.7 = (f32[1536]{0:T(1024)}, f32[1536]{0:T(1024)S(1)}, u32[]{:S(2)}) copy-start(f32[1536]{0:T(1024)S(1)} %reduce.7) | copy-start | bytes 18436
  78.3 308.7 %copy-start.12 = (f32[128]{0:T(128)}, f32[128]{0:T(128)S(1)}, u32[]{:S(2)}) copy-start(f32[128]{0:T(128)S(1)} %add_rsqrt_fusion) | copy-start | bytes 1540
  433.6 2.5 copy-start.2
  470.2 2.5 copy-start.2
  489.5 7.0 %copy-start.3 = (bf16[512,4096]{0,1:T(8,128)(2,1)S(1)}, bf16[512,4096]{0,1:T(8,128)(2,1)}, u32[]{:S(2)}) copy-start(bf16[512,4096]{0,1:T(8,128)(2,1)} %copy.46) | copy-start | bytes 12582916
  503.9 1.0 copy-start.4
  506.3 88.1 %copy-start.6 = (bf16[128,1536]{1,0:T(8,128)(2,1)S(1)}, bf16[128,1536]{1,0:T(8,128)(2,1)}, u32[]{:S(2)}) copy-start(bf16[128,1536]{1,0:T(8,128)(2,1)} %param.15) | copy-start | bytes 1179652
  506.3 88.1 %copy-start.8 = (f32[1536]{0:T(1024)S(1)}, f32[1536]{0:T(1024)}, u32[]{:S(2)}) copy-start(f32[1536]{0:T(1024)} %copy-done.7) | copy-start | bytes 18436
  506.3 88.1 %copy-start.10 = (f32[1536]{0:T(1024)S(1)}, f32[1536]{0:T(1024)}, u32[]{:S(2)}) copy-start(f32[1536]{0:T(1024)} %param.17) | copy-start | bytes 18436
  506.3 91.3 %copy-start.1 = (bf16[128,4096]{1,0:T(8,128)(2,1)S(1)}, bf16[128,4096]{1,0:T(8,128)(2,1)}, u32[]{:S(2)}) copy-start(bf16[128,4096]{1,0:T(8,128)(2,1)} %param.24) | copy-start | bytes 3145732
Sparse Core Ops, SparseCore 0:
  9.5 367.2 all-gather.4
  378.9 39.6 all-gather.2
  520.6 73.7 all-reduce.1
where the time goes:
time: 605 us; the launch traced here: 604 us
  waiting for transfers between devices  388 us (64%)
  matrix products  73.8 us (12%)
  blocking collectives  54.1 us (9%)
  local copies, waits for them, and re-layouts  42.6 us (7%)
  other arithmetic  19.1 us (3%)
  between operations  13.9 us (2%)
  loops' own time  12.1 us (2%)
    all_gather x1, waiting for transfers between devices, shards(): full_wq = lax.all_gather(w_q, 'ctx', axis=0, tiled=True)  298 us
    psum x1, waiting for transfers between devices, shards(): lax.psum(partial_grad.astype(jnp.bfloat16), 'head').astype(jnp.float32)  69.5 us
    all_gather x1, blocking collectives, shards(): rope_portion = lax.all_gather(key_rope, 'ctx', axis=0, tiled=True)  54.1 us
    dot_general x7, matrix products, contract_last(): lax.dot_general(left, right, (((1,), (1,)), ((), ())), preferred_element_...  30.3 us
    dot_general x2, matrix products, update(): jnp.dot(stacked, lat_tile, preferred_element_type=jnp.float32)  21.7 us
    all_gather x1, waiting for transfers between devices, shards(): lat_portion = lax.all_gather(kv_latent, 'ctx', axis=0, tiled=True)  18.9 us
  transfers between devices with their start and end apart: 3, of which 3 were waited for; matrix products, arithmetic and copies ran while one was open for 7% of the time, Pallas kernels for 0%

commit v1 on v0

--- a/solution.py
+++ b/solution.py
@@ -67,8 +67,11 @@
         jnp.zeros((2 * row_count, KVL), jnp.float32),
         jnp.zeros((2 * row_count, ROPE), jnp.float32),
     )
-    lat_portion = lax.all_gather(kv_latent, "ctx", axis=0, tiled=True)
-    rope_portion = lax.all_gather(key_rope, "ctx", axis=0, tiled=True)
+    lat_portion, rope_portion = jnp.split(
+        lax.all_gather(jnp.concatenate([kv_latent, key_rope], axis=1), "ctx", axis=0, tiled=True),
+        [kv_latent.shape[1]],
+        axis=1,
+    )
     key_total = lat_portion.shape[0]
     tile_len = math.gcd(key_total, BLK)
     tile_count = key_total // tile_len

time: 605 us -> 627 us (1.036)
  waiting for transfers between devices: 388 us -> 460 us
  blocking collectives: 54.1 us -> 0 us
    all_gather x1, waiting for transfers between devices: 298 us -> 360 us  [shards(): full_wq = lax.all_gather(w_q, 'ctx', axis=0, tiled=True)]
    all_gather x1 -> x0, blocking collectives: 54.1 us -> none  [shards(): rope_portion = lax.all_gather(key_rope, 'ctx', axis=0, tiled=True)]
    all_gather x1, waiting for transfers between devices: 18.9 us -> 28.9 us  [shards(): lax.all_gather(jnp.concatenate([kv_latent, key_rope], axis=1), 'ctx', axi...]
  transfers between devices with their start and end apart: 3 -> 3, of which waited for: 3 -> 3; matrix products, arithmetic and copies ran while one was open for 7% -> 4% of each run, Pallas kernels for 0% -> 0%
where the time goes in v1:
time: 627 us; the launch traced here: 626 us
  waiting for transfers between devices  460 us (73%)
  matrix products  71 us (11%)
  local copies, waits for them, and re-layouts  46.6 us (7%)
  other arithmetic  20.9 us (3%)
  between operations  14 us (2%)
  loops' own time  12.7 us (2%)
    all_gather x1, waiting for transfers between devices, shards(): full_wq = lax.all_gather(w_q, 'ctx', axis=0, tiled=True)  360 us
    psum x1, waiting for transfers between devices, shards(): lax.psum(partial_grad.astype(jnp.bfloat16), 'head').astype(jnp.float32)  71.3 us
    all_gather x1, waiting for transfers between devices, shards(): lax.all_gather(jnp.concatenate([kv_latent, key_rope], axis=1), 'ctx', axi...  28.9 us
    dot_general x7, matrix products, contract_last(): lax.dot_general(left, right, (((1,), (1,)), ((), ())), preferred_element_...  27.6 us
    dot_general x2, matrix products, update(): jnp.dot(stacked, lat_tile, preferred_element_type=jnp.float32)  21.7 us
  transfers between devices with their start and end apart: 3, of which 3 were waited for; matrix products, arithmetic and copies ran while one was open for 4% of the time, Pallas kernels for 0%

profile of v1, /device:TPU:0, one launch (start us, length us, event | category | flops | bytes accessed | tf_op | source)
XLA Modules:
  0.0 625.7 jit_solution(10141913895870668804)
XLA Ops:
  7.2 0.9 copy.32
  8.1 1.6 pad_maximum_fusion.5
  9.8 0.7 all-gather.5.cloned.1.call-update
  10.6 6.5 %copy.46 = bf16[512,4096]{0,1:T(8,128)(2,1)} copy(bf16[512,4096]{1,0:T(8,128)(2,1)} %param.22) | data formatting | bytes 8388608 | tf_op jit(solution)/shard_map/reshape | solution.py:43
  17.0 3.5 convert_bitcast_fusion.1
  20.5 4.4 copy.40
  25.0 0.7 constant_dynamic-slice_fusion.1
  25.9 28.9 %all-gather.3.cloned.1.call-done = bf16[1024,576]{1,0:T(8,128)(2,1)} async-done(((bf16[128,576]{1,0:T(8,128)(2,1)}), bf16[1024,576]{1,0:T(8,128)(2,1)}) %all-gather.3.cloned.1.call-update) | async-done | bytes 1179664 | tf_op jit(solution)/shard_map/all_gather | solution.py:71
  54.8 1.0 split.9
  55.7 2.3 split.8
  58.0 359.5 %all-gather.5.cloned.1.call-done = bf16[1536,6144]{1,0:T(8,128)(2,1)} async-done(((bf16[192,6144]{1,0:T(8,128)(2,1)}), bf16[1536,6144]{1,0:T(8,128)(2,1)}) %all-gather.5.cloned.1.call-update) | async-done | bytes 18874384 | tf_op jit(solution)/shard_map/all_gather | solution.py:35
  417.6 10.2 %fusion.23 = bf16[128,6144]{1,0:T(8,128)(2,1)} fusion(bf16[1536,6144]{1,0:T(8,128)(2,1)} %all-gather.5.cloned.1.call-done, f32[6144]{0:T(1024)S(1)} %bitcast.80, bf16[128,1536]{1,0:T(8,128)(2,1)S(1)} %copy-done.5, f32[1536]{0:T(1024)S(1)} %copy-done.9, f32[128]{0:T(128)S(1)} %add_rsqrt_fusion, f32[1536]{0:T(1024)S(1)} %reduce.7), kind=kOutput, calls=%fused_computation.37 | convolution fusion | flops 2418475008 | bytes 20877824 | tf_op jit(solution)/shard_map/dot_general | solution.py:36
  427.8 2.1 copy.33
  429.9 1.6 copy.37
  431.6 3.5 convert_bitcast_fusion.2
  435.0 4.5 copy.36
  439.7 7.9 %broadcast_in_dim.47 = f32[8192,512]{1,0:T(8,128)} broadcast(f32[]{:T(128)} %constant.105.clone.1), dimensions={} | broadcast | bytes 16777220 | tf_op jit(solution)/shard_map/broadcast_in_dim | solution.py:67
  447.6 63.6 %while.20 = (s32[]{:T(128)}, f32[4096]{0:T(1024)S(1)}, f32[4096]{0:T(1024)S(1)}, f32[4096]{0:T(1024)S(1)}, f32[8192,512]{1,0:T(8,128)}, /*index=5*/f32[8192,64]{...) while((s32[]{:T(128)}, f32[4096]{0:T(1024)S(1)}, ...), condition=%wide.region_7.8_spmd, body=%wide.region_1.7_spmd.sunk | while | flops 2372423680 | bytes 79530632 | solution.py:119
  449.0 0.7 fusion.59
  450.3 20.9 %conditional.2 = ((f32[4096]{0:T(1024)S(1)}, f32[4096]{0:T(1024)S(1)}, f32[4096]{0:T(1024)S(1)}, f32[8192,512]{1,0:T(8,128)}, f32[8192,64]{0,1:T(8,128)S(1)})) conditional(s32[]{:T(128)} %bitcast.67, (f32[4096]{0:T(1024)S(1)}, f32[4096]{0:T(1024)S(1)}, f32[4096]{0:T(1024)S(1)}, f32[8192,512]{1,0:T(8,128)}, f32[8192,64]{0,1:T(8,128)S(1)}) %tuple.55, ...), branch_computations={%region_2.2_spmd, %region_3.6_spmd} | conditional | flops 2372423680 | bytes 79530080 | solution.py:111
  451.0 3.7 fusion.7
  455.3 1.6 copy-done.2
  456.9 2.5 fusion.4
  459.4 0.9 convolution_add_fusion
  460.3 10.9 %multiply_add_fusion = f32[8192,512]{1,0:T(8,128)} fusion(f32[8192,512]{1,0:T(8,128)} %get-tuple-element.261, f32[8192]{0:T(1024)S(1)} %pad_maximum_fusion.3, bf16[4096,128]{0,1:T(8,128)(2,1)S(1)} %get-tuple-element.320, bf16[4096,128]{0,1:T(8,128)(2,1)S(1)} %get-tuple-element.327, bf16[8,128,512]{2,1,0:T(8,128)(2,1)} %get-tuple-element.253, ...), kind=kOutput, calls=%fused_computation | convolution fusion | flops 1086324736 | bytes 35815936 | tf_op jit(solution)/shard_map/while/body/eval_jaxpr/cond/branch_1_fun/dot_general | solution.py:100
  472.6 0.7 fusion.59
  475.3 0.7 fusion.59
  478.0 0.7 fusion.59
  480.7 0.7 fusion.59
  483.5 0.7 fusion.59
  486.2 0.7 fusion.59
  487.5 20.9 %conditional.2 = ((f32[4096]{0:T(1024)S(1)}, f32[4096]{0:T(1024)S(1)}, f32[4096]{0:T(1024)S(1)}, f32[8192,512]{1,0:T(8,128)}, f32[8192,64]{0,1:T(8,128)S(1)})) conditional(s32[]{:T(128)} %bitcast.67, (f32[4096]{0:T(1024)S(1)}, f32[4096]{0:T(1024)S(1)}, f32[4096]{0:T(1024)S(1)}, f32[8192,512]{1,0:T(8,128)}, f32[8192,64]{0,1:T(8,128)S(1)}) %tuple.55, ...), branch_computations={%region_2.2_spmd, %region_3.6_spmd} | conditional | flops 2372423680 | bytes 79530080 | solution.py:111
  488.2 3.7 fusion.7
  492.5 1.6 copy-done.2
  494.1 2.5 fusion.4
  496.7 0.9 convolution_add_fusion
  497.6 10.9 %multiply_add_fusion = f32[8192,512]{1,0:T(8,128)} fusion(f32[8192,512]{1,0:T(8,128)} %get-tuple-element.261, f32[8192]{0:T(1024)S(1)} %pad_maximum_fusion.3, bf16[4096,128]{0,1:T(8,128)(2,1)S(1)} %get-tuple-element.320, bf16[4096,128]{0,1:T(8,128)(2,1)S(1)} %get-tuple-element.327, bf16[8,128,512]{2,1,0:T(8,128)(2,1)} %get-tuple-element.253, ...), kind=kOutput, calls=%fused_computation | convolution fusion | flops 1086324736 | bytes 35815936 | tf_op jit(solution)/shard_map/while/body/eval_jaxpr/cond/branch_1_fun/dot_general | solution.py:100
  511.2 6.9 %multiply_convert_fusion = bf16[4096,512]{1,0:T(8,128)(2,1)S(1)} fusion(f32[8192,512]{1,0:T(8,128)} %get-tuple-element.288, f32[4096]{0:T(1024)S(1)} %get-tuple-element.331, f32[4096]{0:T(1024)S(1)} %get-tuple-element.330), kind=kLoop, calls=%fused_computation.35 | loop fusion | flops 8388608 | bytes 21004288 | tf_op jit(solution)/shard_map/convert_element_type | solution.py:123
  518.2 2.8 fusion.33
  521.0 2.0 copy.43
  523.0 2.7 copy.44
  525.7 1.4 fusion.31
  527.2 14.1 %convolution_convert_fusion = bf16[128,1536]{1,0:T(8,128)(2,1)} fusion(bf16[128,6144]{0,1:T(8,128)(2,1)} %bitcast.78, bf16[1536,6144]{1,0:T(8,128)(2,1)} %all-gather.5.cloned.1.call-done), kind=kOutput, calls=%fused_computation.48 | convolution fusion | flops 2416115712 | bytes 20840448 | tf_op jit(solution)/shard_map/dot_general | solution.py:17
  541.3 2.8 fusion.32
  544.0 0.7 reduce_sum.64
  544.7 71.3 %all-reduce.2.cloned.1.call-done = bf16[128,1536]{1,0:T(8,128)(2,1)} async-done(((bf16[128,1536]{1,0:T(8,128)(2,1)}), bf16[128,1536]{1,0:T(8,128)(2,1)}) %all-reduce.2.cloned.1.call-update) | async-done | bytes 393232 | tf_op jit(solution)/shard_map/psum | solution.py:137
  616.0 1.3 multiply_reduce_fusion.1
  617.3 1.3 multiply_reduce_fusion
  (75 shorter events, 8.5 us)
Async XLA Ops:
  7.2 9.9 %copy-start = (bf16[128,4096]{1,0:T(8,128)(2,1)S(1)}, bf16[128,4096]{1,0:T(8,128)(2,1)}, u32[]{:S(2)}) copy-start(bf16[128,4096]{1,0:T(8,128)(2,1)} %param.24) | copy-start | bytes 3145732
  7.2 47.6 %all-gather.3.cloned.1.call-start = ((), (), s32[]{:S(2)}) async-start(), calls=%async_computation | async-start | bytes 1474560 | tf_op jit(solution)/shard_map/all_gather | solution.py:71
  9.8 407.8 %all-gather.5.cloned.1.call-start = ((), (), s32[]{:S(2)}) async-start(), calls=%async_computation.1 | async-start | bytes 21233664 | tf_op jit(solution)/shard_map/all_gather | solution.py:35
  10.5 605.5 %all-reduce.2.cloned.1.call-start = ((), (), s32[]{:S(2)}) async-start(), calls=%async_computation.2 | async-start | bytes 786432 | tf_op jit(solution)/shard_map/psum | solution.py:137
  20.5 4.4 copy-start.14
  20.5 5.1 copy-start.5
  20.5 397.0 %copy-start.9 = (f32[1536]{0:T(1024)S(1)}, f32[1536]{0:T(1024)}, u32[]{:S(2)}) copy-start(f32[1536]{0:T(1024)} %param.17) | copy-start | bytes 18436
  20.5 397.0 %copy-start.11 = (f32[1,6144]{1,0:T(1,128)S(1)}, f32[1,6144]{1,0:T(1,128)}, u32[]{:S(2)}) copy-start(f32[1,6144]{1,0:T(1,128)} %param.19) | copy-start | bytes 73732
  24.9 402.8 %copy-start.7 = (f32[1536]{0:T(1024)}, f32[1536]{0:T(1024)S(1)}, u32[]{:S(2)}) copy-start(f32[1536]{0:T(1024)S(1)} %reduce.7) | copy-start | bytes 18436
  25.8 401.9 %copy-start.12 = (f32[128]{0:T(128)}, f32[128]{0:T(128)S(1)}, u32[]{:S(2)}) copy-start(f32[128]{0:T(128)S(1)} %add_rsqrt_fusion) | copy-start | bytes 1540
  454.7 2.2 copy-start.2
  492.0 2.2 copy-start.2
  511.2 7.0 %copy-start.3 = (bf16[512,4096]{0,1:T(8,128)(2,1)S(1)}, bf16[512,4096]{0,1:T(8,128)(2,1)}, u32[]{:S(2)}) copy-start(bf16[512,4096]{0,1:T(8,128)(2,1)} %copy.46) | copy-start | bytes 12582916
  521.0 6.1 copy-start.4
  527.1 88.9 %copy-start.6 = (bf16[128,1536]{1,0:T(8,128)(2,1)S(1)}, bf16[128,1536]{1,0:T(8,128)(2,1)}, u32[]{:S(2)}) copy-start(bf16[128,1536]{1,0:T(8,128)(2,1)} %param.15) | copy-start | bytes 1179652
  527.1 88.9 %copy-start.8 = (f32[1536]{0:T(1024)S(1)}, f32[1536]{0:T(1024)}, u32[]{:S(2)}) copy-start(f32[1536]{0:T(1024)} %copy-done.7) | copy-start | bytes 18436
  527.1 88.9 %copy-start.10 = (f32[1536]{0:T(1024)S(1)}, f32[1536]{0:T(1024)}, u32[]{:S(2)}) copy-start(f32[1536]{0:T(1024)} %param.17) | copy-start | bytes 18436
  527.1 88.9 %copy-start.13 = (f32[128]{0:T(128)S(1)}, f32[128]{0:T(128)}, u32[]{:S(2)}) copy-start(f32[128]{0:T(128)} %copy-done.12) | copy-start | bytes 1540
  527.1 92.1 %copy-start.1 = (bf16[128,4096]{1,0:T(8,128)(2,1)S(1)}, bf16[128,4096]{1,0:T(8,128)(2,1)}, u32[]{:S(2)}) copy-start(bf16[128,4096]{1,0:T(8,128)(2,1)} %param.24) | copy-start | bytes 3145732
Sparse Core Ops, SparseCore 0:
  10.2 44.5 all-gather.2
  56.3 361.2 all-gather.4
  541.4 74.5 all-reduce.1
